TPU v7x, 128 devices: a whole 4x4x4 slice. The times are simulated.
128 devices in a mesh: req: 16 (over x, y), exp: 8 (over z, core).
Axes of the slice: x: 4, y: 4, z: 4, core: 2. Of those that a mesh axis runs over, the one named last changes fastest.
Arguments:
- tokens: bfloat16 [16384, 2048], P(('req', 'exp')), may hold values from -6 to 6
- attn_gain: float32 [2048], replicated, may hold values from 0.1 to 1.9
- w_query: bfloat16 [2048, 2048], P(None, 'exp'), may hold values from -0.25 to 0.25
- w_key: bfloat16 [2048, 2048], P(None, 'exp'), may hold values from -0.125 to 0.125
- w_value: bfloat16 [2048, 2048], P(None, 'exp'), may hold values from -0.125 to 0.125
- w_out: bfloat16 [2048, 2048], P('exp'), may hold values from -0.375 to 0.375
- prefix_cache: bfloat16 [8, 1024, 2, 2048], P(None, 'req', None, 'exp'), may hold values from -205 to 205
- group_of: int32 [16], replicated, may hold values from 0 to 7
- lengths: int32 [16], replicated, may hold values from 1 to 1024, 10240 in all
- moe_gain: float32 [2048], replicated, may hold values from 0.1 to 1.9
- w_gate: bfloat16 [128, 2048, 512], P(('req', 'exp')), may hold values from -0.125 to 0.125
- w_up: bfloat16 [128, 2048, 512], P(('req', 'exp')), may hold values from -0.125 to 0.125
- w_down: bfloat16 [128, 512, 2048], P(('req', 'exp')), may hold values from -0.25 to 0.25
- routes: int32 [16384, 8], P(('req', 'exp')), may hold values from 0 to 63, all different within a row; in each aligned block of 128 rows (0 to 127, 128 to 255, ...) at most 18 rows name the same one
- route_weights: float32 [16384, 8], P(('req', 'exp')), may hold values from 0.1 to 0.4
Outputs:
- layer_out: bfloat16 [16384, 2048], P(('req', 'exp'))
Inputs may be any that keep to these rules, and one draw needn't show every extreme that they name: `routes`: in the rows of one device no expert is named more than 18 times.
All inputs are finite; a program needn't handle non-finite values.
Results may differ from a plain program's by a relative error of at most 0.017.
Values may be sent and summed in bfloat16 or wider, within the bound.
No kernel may reach another device: no remote copies, remote signals or barrier semaphores. Data moves between devices by JAX's collectives and lax.ppermute only.
A program may use at most 192 MiB of HBM per device.

v0:
```python
import functools
import math

import jax
import jax.numpy as jnp
import numpy as np
from jax import lax
from jax.experimental import pallas as pl
from jax.experimental.pallas import tpu as pltpu
from jax.sharding import Mesh
from jax.sharding import PartitionSpec as P


HD = 128
PREFIX = 1024
BF = jnp.bfloat16
F32 = jnp.float32
SUB = 8


def vmem():
    return pl.BlockSpec(memory_space=pltpu.VMEM)


def limit(mib):
    return pltpu.CompilerParams(vmem_limit_bytes=mib << 20)


def smem():
    return pl.BlockSpec(memory_space=pltpu.SMEM)


def call(kernel, out_shape, n_in, mib=16, **kw):
    outs = jax.tree.map(lambda _: vmem(), out_shape)
    return pl.pallas_call(
        kernel, out_shape=out_shape, in_specs=[vmem()] * n_in, out_specs=outs,
        compiler_params=limit(mib), **kw
    )


def near(a):
    return pltpu.with_memory_space_constraint(a, pltpu.VMEM)


def away(a):
    return pltpu.with_memory_space_constraint(a, pltpu.HBM)


def shape(dims, dtype):
    return jax.ShapeDtypeStruct(dims, dtype)


def dot(a, b):
    return jnp.dot(a, b, preferred_element_type=F32)


def rms(wide, gain):
    return wide * lax.rsqrt(jnp.mean(wide * wide, axis=-1, keepdims=True) + 1e-05) * gain


def norm_kernel(x_ref, g_ref, o_ref, first_ref, last_ref):
    normed = rms(x_ref[...].astype(F32), g_ref[...]).astype(BF)
    o_ref[...] = normed
    half = first_ref.shape[0]
    first_ref[...] = normed[:half]
    last_ref[...] = normed[half:]


def seat():
    req = lax.axis_index("x") * lax.axis_size("y") + lax.axis_index("y")
    return req, lax.axis_index("z"), lax.axis_index("c")


def held_blocks():
    _, z, core = seat()
    zs = lax.axis_size("z")
    chips = [lax.rem(z + d, zs) for d in (0, zs - 1, 1, 2)]
    return [chip * 2 + who for who in (core, 1 - core) for chip in chips]


def tables(rows, blocks):
    freqs = 10000.0 ** (-(np.arange(HD // 2) * 2.0) / HD)
    freqs = np.concatenate([freqs, freqs])
    first = (PREFIX + rows * np.arange(blocks))[:, None] * freqs
    within = np.arange(rows)[:, None] * freqs
    return [f(a).astype(np.float32) for a in (first, within) for f in (np.cos, np.sin)]


def slots_of(index):
    block = index // SUB
    return block // 2, (block % 2) * (SUB + 1) + index % SUB


def route_kernel(zs, len_ref, rt_ref, wt_ref, dt_ref, wm_ref, wx_ref, live_ref, order_ref):
    top, rows = rt_ref.shape
    req, z, core = seat()
    row = lax.broadcasted_iota(jnp.int32, live_ref.shape, 0)
    live_ref[...] = jnp.where(row < len_ref[req] - (z * 2 + core) * rows, 1.0, 0.0)
    senders = order_ref.shape[0] - 1

    def pick(wanted):
        def step(s, n):
            full = len_ref[s // zs] > (s % zs * 2 + core) * rows
            take = full == wanted

            @pl.when(take)
            def _():
                order_ref[n] = s

            return n + take.astype(jnp.int32)

        return step

    count = lax.fori_loop(0, senders, pick(True), jnp.int32(0))
    order_ref[senders] = count
    lax.fori_loop(0, senders, pick(False), count)
    blocks = wx_ref.shape[1]
    experts = blocks // 2
    wide = blocks * SUB
    iota = lambda dims, axis: lax.broadcasted_iota(jnp.int32, dims, axis)
    one = lambda hit: jnp.where(hit, 1.0, 0.0)
    row_i = iota((rows, rows), 0)
    col_i = iota((rows, rows), 1)
    e_t = iota((experts, rows), 0)
    named_t = jnp.zeros((experts, rows), F32)
    weight_t = jnp.zeros((experts, rows), F32)
    for k in range(top):
        hit = rt_ref[k : k + 1, :] == e_t
        named_t += one(hit)
        weight_t += jnp.where(hit, wt_ref[k : k + 1, :], 0.0)
    rank_t = dot(named_t.astype(BF), one(row_i < col_i).astype(BF))
    rank_t = jnp.where(named_t > 0.5, rank_t, -1.0).astype(BF)
    expert, _ = slots_of(iota((wide, experts), 0))
    spread = one(expert == iota((wide, experts), 1)).astype(BF)
    _, slot = slots_of(iota((wide, rows), 0))
    dt_ref[:wide, :] = one(dot(spread, rank_t) == slot.astype(F32)).astype(BF)
    block = iota((blocks, experts), 0)
    spread = one(block // 2 == iota((blocks, experts), 1)).astype(BF)
    slot = (iota((blocks, rows), 0) % 2) * (SUB + 1) + SUB
    dt_ref[wide:, :] = one(dot(spread, rank_t) == slot.astype(F32)).astype(BF)
    named = jnp.transpose(named_t)
    weight = jnp.transpose(weight_t)
    rank = dot(one(col_i < row_i).astype(BF), named.astype(BF))
    rank = jnp.where(named > 0.5, rank, -1.0).astype(BF)
    high = weight.astype(BF)
    low = (weight - high.astype(F32)).astype(BF)
    expert, _ = slots_of(iota((experts, wide), 1))
    spread = one(expert == iota((experts, wide), 0)).astype(BF)
    _, slot = slots_of(iota((rows, wide), 1))
    hit = dot(rank, spread) == slot.astype(F32)
    wm_ref[:rows, :] = jnp.where(hit, dot(high, spread), 0.0).astype(BF)
    wm_ref[rows:, :] = jnp.where(hit, dot(low, spread), 0.0).astype(BF)
    block = iota((experts, blocks), 1)
    spread = one(block // 2 == iota((experts, blocks), 0)).astype(BF)
    slot = (iota((rows, blocks), 1) % 2) * (SUB + 1) + SUB
    hit = dot(rank, spread) == slot.astype(F32)
    wx_ref[:rows, :] = jnp.where(hit, dot(high, spread), 0.0).astype(BF)
    wx_ref[rows:, :] = jnp.where(hit, dot(low, spread), 0.0).astype(BF)


def prefix_kernel(group_ref, x_ref, o_ref):
    rows, width = x_ref.shape[2:]
    for r in range(o_ref.shape[0] // rows):
        for j in range(2):
            o_ref[r * rows : (r + 1) * rows, j * width : (j + 1) * width] = x_ref[group_ref[r], j]


def qkv_kernel(count, *refs):
    pieces, weights, refs = refs[:count], refs[count : count + 6], refs[count + 6 :]
    len_hbm, c0_ref, s0_ref, c1_ref, s1_ref, q_ref, k_ref, v_ref, bias_ref = refs[:9]
    x_ref, w_ref, cos_ref, sin_ref, len_ref, x_sem, w_sem, len_sem = refs[9:]
    at = 0
    copies = []
    for i, piece in enumerate(pieces):
        n = piece.shape[0]
        copies.append(pltpu.make_async_copy(piece, x_ref.at[at : at + n], x_sem.at[i]))
        at += n
    local = w_ref.shape[2] // 2
    loads = [
        pltpu.make_async_copy(
            w, w_ref.at[i // 2, :, i % 2 * local : (i % 2 + 1) * local], w_sem.at[i]
        )
        for i, w in enumerate(weights)
    ]
    early = len(copies) // 2
    for copy in (*loads[:2], *copies[:early], *loads[2:], *copies[early:]):
        copy.start()
    facts = pltpu.make_async_copy(len_hbm, len_ref, len_sem)
    facts.start()
    n = c1_ref.shape[0]
    side = jnp.where(lax.broadcasted_iota(jnp.int32, (n, HD), 1) < HD // 2, -1.0, 1.0)
    for i, block in enumerate(held_blocks()):
        c0, s0 = c0_ref[pl.ds(block, 1), :], s0_ref[pl.ds(block, 1), :]
        here = slice(i * n, (i + 1) * n)
        if i == 0:
            facts.wait()
            req, _, _ = seat()
            lane = lax.broadcasted_iota(jnp.int32, (1, n), 1)
        bias_ref[:, here] = jnp.where(block * n + lane < len_ref[req], 0.0, -1e30)
        cos_ref[here, :] = c0 * c1_ref[...] - s0 * s1_ref[...]
        sin_ref[here, :] = side * (s0 * c1_ref[...] + c0 * s1_ref[...])
    half = q_ref.shape[0]
    at, left = 0, list(copies)
    for rows in (slice(0, half), slice(half, 2 * half)):
        while at < rows.stop:
            left.pop(0).wait()
            at += pieces[len(pieces) - len(left) - 1].shape[0]
        for i, o_ref in enumerate((k_ref, q_ref, v_ref)):
            if rows.start == 0:
                loads[2 * i].wait()
                loads[2 * i + 1].wait()
            elif o_ref is q_ref:
                continue
            mixed = dot(x_ref[rows, :], w_ref[i])
            if o_ref is v_ref:
                o_ref[rows, :] = mixed.astype(BF)
                continue
            for h in range(2 * local // HD):
                v = mixed[:, h * HD : (h + 1) * HD]
                turned = v * cos_ref[rows, :] + pltpu.roll(v, HD // 2, 1) * sin_ref[rows, :]
                o_ref[rows, h * HD : (h + 1) * HD] = turned.astype(BF)


def attend(scale, q_ref, k_ref, v_ref, pre_refs, bias_ref, o_ref, ranges):
    local = pre_refs[0].shape[1] // 2
    nt = (((1,), (1,)), ((), ()))
    for h in range(q_ref.shape[1] // HD):
        side, col = divmod(h * HD, local)
        pre_ref = pre_refs[side]
        cols = slice(h * HD, (h + 1) * HD)
        q = jnp.concatenate([q_ref[at : at + n, cols] for at, n in ranges], axis=0)
        s1 = lax.dot_general(q, pre_ref[:, col : col + HD], nt, preferred_element_type=F32)
        s2 = lax.dot_general(q, k_ref[:, cols], nt, preferred_element_type=F32) + bias_ref[...]
        top = jnp.maximum(
            jnp.max(s1, axis=-1, keepdims=True), jnp.max(s2, axis=-1, keepdims=True)
        )
        e1 = jnp.exp2((s1 - top) * scale)
        e2 = jnp.exp2((s2 - top) * scale)
        total = jnp.sum(e1, axis=-1, keepdims=True) + jnp.sum(e2, axis=-1, keepdims=True)
        out = dot(e1.astype(BF), pre_ref[:, local + col : local + col + HD])
        out += dot(e2.astype(BF), v_ref[:, cols])
        o_ref[:, cols] = (out / total).astype(BF)


def project(a_ref, wa_ref, wb_ref):
    local = wa_ref.shape[0]
    return dot(a_ref[:, :local], wa_ref[...]) + dot(a_ref[:, local:], wb_ref[...])


def attn_pair_kernel(scale, ranges, q, k, v, pa, pb, wa, wb, bias, o1, o2, tmp):
    attend(scale, q, k, v, (pa, pb), bias, tmp, ranges)
    total = project(tmp, wa, wb)
    rows = o1.shape[0]
    o1[...] = total[:rows].astype(o1.dtype)
    o2[...] = total[rows:].astype(o2.dtype)


def attn_own_kernel(scale, ranges, q, k, v, pa, pb, wa, wb, bias, o, tmp):
    attend(scale, q, k, v, (pa, pb), bias, tmp, ranges)
    o[...] = project(tmp, wa, wb)


def add_kernel(a_ref, a_got, b_ref, b_got, a_out, b_out):
    a_out[...] = (a_ref[...] + a_got[...].astype(F32)).astype(BF)
    b_out[...] = (b_ref[...] + b_got[...].astype(F32)).astype(BF)


def dispatch_kernel(t_ref, own_ref, a1, a2, b1, b2, g_ref, d_ref, h_ref, o_ref, normed, extra):
    half = a1.shape[0]
    width = t_ref.shape[1]
    part = width // SUB
    wide = o_ref.shape[0]
    blocks = wide // SUB
    for at, x, y in ((0, a1, a2), (half, b1, b2)):
        here = slice(at, at + half)
        attn_out = own_ref[here, :] + x[...].astype(F32) + y[...].astype(F32)
        hidden = (t_ref[here, :].astype(F32) + attn_out).astype(BF)
        h_ref[here, :] = hidden
        normed[here, :] = rms(hidden.astype(F32), g_ref[...]).astype(BF)
    for b in range(0, SUB, 2):
        x = normed[:, b * part : (b + 2) * part]
        o_ref[:, b * part : (b + 2) * part] = dot(d_ref[:wide, :], x).astype(BF)
        more = dot(d_ref[wide:, :], x)
        for n in range(2 * part // 128):
            row, i = divmod(n, part // 128)
            extra[i, pl.ds(b + row, blocks, stride=SUB), :] = more[:, n * 128 : (n + 1) * 128]
    for i in range(part // 128):
        o_ref[:, width + i * 128 : width + (i + 1) * 128] = extra[i].astype(BF)


def dispatch(tokens, *rest):
    args = (tokens, *rest)
    rows, width = tokens.shape
    part = width // SUB
    wide = rest[-1].shape[0] // (SUB + 1) * SUB
    return call(
        dispatch_kernel,
        (pltpu.HBM((rows, width), BF), pltpu.VMEM((wide, width + part), BF)),
        len(args),
        scratch_shapes=[
            pltpu.VMEM((rows, width), BF), pltpu.VMEM((part // 128, wide, 128), F32),
        ],
        name="dispatch",
    )(*args)


def ffn_kernel(group, order_ref, x_ref, *refs):
    weights = refs[:3], refs[3:6]
    o_ref, rows_ref, act, extra = refs[6:]
    senders, each = x_ref.shape[:2]
    width = rows_ref.shape[1]
    part = width // SUB
    wide = group * each
    blocks = wide // SUB
    hidden = act.shape[1] // 2
    steps = (order_ref[senders] + group - 1) // group

    def body(j, carry):
        for s in range(group):
            x = x_ref.at[order_ref[j * group + s]]
            here = slice(s * each, (s + 1) * each)
            rows_ref[here, :] = x[:, :width]
            for i in range(part // 128):
                extra[i, here, :] = x[:, width + i * 128 : width + (i + 1) * 128].astype(F32)
        for b in range(SUB):
            for i in range(part // 128):
                col = b * part + i * 128
                rows_ref[wide:, col : col + 128] = extra[i, pl.ds(b, blocks, stride=SUB), :].astype(
                    BF
                )
        for h, (g_ref, u_ref, _) in enumerate(weights):
            gate = dot(rows_ref[...], g_ref[...])
            silu = 0.5 * gate * (1.0 + jnp.tanh(0.5 * gate))
            upper = dot(rows_ref[...], u_ref[...])
            act[:, h * hidden : (h + 1) * hidden] = (silu * upper).astype(BF)
        total = dot(act[:, :hidden], weights[0][2][...])
        total += dot(act[:, hidden:], weights[1][2][...])
        for b in range(SUB):
            for i in range(part // 128):
                col = b * part + i * 128
                extra[i, pl.ds(b, blocks, stride=SUB), :] = total[wide:, col : col + 128]
        for s in range(group):
            o = o_ref.at[order_ref[j * group + s]]
            here = slice(s * each, (s + 1) * each)
            o[:, :width] = total[here].astype(BF)
            for i in range(part // 128):
                o[:, width + i * 128 : width + (i + 1) * 128] = extra[i, here, :].astype(BF)
        return carry

    lax.fori_loop(0, steps, body, 0)


def ffn(order, x, w0, w1):
    width, hidden = w0[0].shape
    each = x.shape[1]
    group = 16
    wide = group * each
    rows = wide + wide // SUB
    return pl.pallas_call(
        functools.partial(ffn_kernel, group),
        out_shape=pltpu.VMEM(x.shape, BF),
        in_specs=[smem()] + [vmem()] * 7,
        out_specs=vmem(),
        scratch_shapes=[
            pltpu.VMEM((rows, width), BF),
            pltpu.VMEM((rows, 2 * hidden), BF),
            pltpu.VMEM((width // SUB // 128, wide, 128), F32),
        ],
        compiler_params=limit(24),
        name="ffn",
    )(order, *map(near, (x, *w0, *w1)))


def combine_kernel(r_ref, wm_ref, wx_ref, h_ref, live_ref, o_ref, extra):
    rows, width = o_ref.shape
    part = width // SUB
    blocks = r_ref.shape[0] // SUB
    live = jnp.concatenate([live_ref[...]] * (2 * part // live_ref.shape[1]), axis=1) > 0.5
    for i in range(part // 128):
        extra[i] = r_ref[:, width + i * 128 : width + (i + 1) * 128].astype(F32)
    for b in range(0, SUB, 2):
        cols = slice(b * part, (b + 2) * part)
        more = [
            extra[i, pl.ds(b + n, blocks, stride=SUB), :]
            for n in range(2)
            for i in range(part // 128)
        ]
        more = jnp.concatenate(more, axis=1).astype(BF)
        both = dot(wm_ref[...], r_ref[:, cols]) + dot(wx_ref[...], more)
        out = h_ref[:, cols].astype(F32) + both[:rows] + both[rows:]
        o_ref[:, cols] = jnp.where(live, out, 0.0).astype(BF)


def combine(live, back, wm, wx, hidden):
    part = hidden.shape[1] // SUB
    return call(
        combine_kernel,
        shape(hidden.shape, BF),
        5,
        scratch_shapes=[pltpu.VMEM((part // 128, back.shape[0], 128), F32)],
        name="combine",
    )(near(back), wm, wx, hidden, live)


def layer(
    tokens, attn_gain, w_query, w_key, w_value, w_out, prefix_cache, group_of, lengths,
    moe_gain, w_gate, w_up, w_down, routes, route_weights,
):
    rows, width = tokens.shape
    zs = lax.axis_size("z")
    reqs = lax.axis_size("x") * lax.axis_size("y")
    experts = reqs * zs
    local = w_query.shape[1]
    up = [(i, (i + 1) % zs) for i in range(zs)]
    down = [(i, (i - 1) % zs) for i in range(zs)]
    swap = lambda v: lax.ppermute(v, "c", [(0, 1), (1, 0)])
    to_up = lambda v: lax.ppermute(v, "z", up)
    to_down = lambda v: lax.ppermute(v, "z", down)
    half = rows // 2

    part = pltpu.HBM((half, width), BF)
    normed, first, last = call(
        norm_kernel, (pltpu.HBM((rows, width), BF), part, part), 2, name="norm"
    )(away(tokens), away(attn_gain[None]))
    low0 = to_up(first)
    high1 = to_down(last)
    low1 = to_up(last)
    high0 = to_down(first)
    own_b = swap(normed)
    far0 = to_up(low0)
    far1 = to_down(high1)
    near_a = (low0, low1, high0, high1)
    near_b = tuple(swap(v) for v in near_a)

    wk = (w_key, swap(w_key))
    wq = (w_query, swap(w_query))
    wv = (w_value, swap(w_value))
    out_b = swap(w_out)

    spread = prefix_cache.shape[1]
    outgoing = pl.pallas_call(
        prefix_kernel,
        out_shape=pltpu.HBM((reqs * spread, 2 * local), BF),
        in_specs=[pl.BlockSpec(memory_space=pltpu.SMEM), vmem()],
        out_specs=vmem(),
        compiler_params=limit(16),
        name="prefix",
    )(away(group_of), jnp.transpose(prefix_cache, (0, 2, 1, 3)))
    pre_a = lax.all_to_all(outgoing, ("x", "y"), split_axis=0, concat_axis=0, tiled=True)
    pre_b = swap(pre_a)

    own_w = (w_gate[0], w_up[0], w_down[0])
    other_w = tuple(swap(w) for w in own_w)

    far_b = swap(far0), swap(far1)


    slots = 2 * zs * rows
    pieces = (normed, *near_a, far0, far1, own_b, *near_b, *far_b)
    q, k, v, bias = pl.pallas_call(
        lambda *refs: qkv_kernel(len(pieces), *refs),
        out_shape=(
            pltpu.VMEM((slots // 2, 2 * local), BF),
            pltpu.VMEM((slots, 2 * local), BF),
            pltpu.VMEM((slots, 2 * local), BF),
            pltpu.VMEM((1, slots), F32),
        ),
        in_specs=[pl.BlockSpec(memory_space=pl.ANY)] * (len(pieces) + 7) + [vmem()] * 4,
        out_specs=(vmem(),) * 4,
        scratch_shapes=[
            pltpu.VMEM((slots, width), BF),
            pltpu.VMEM((3, width, 2 * local), BF),
            pltpu.VMEM((slots, HD), F32),
            pltpu.VMEM((slots, HD), F32),
            pltpu.SMEM(lengths.shape, jnp.int32),
            pltpu.SemaphoreType.DMA((len(pieces),)),
            pltpu.SemaphoreType.DMA((6,)),
            pltpu.SemaphoreType.DMA(()),
        ],
        compiler_params=limit(24),
        name="qkv",
    )(*map(away, (*pieces, *wk, *wq, *wv, lengths, *map(jnp.asarray, tables(rows, 2 * zs)))))
    cache = (near(q), near(k), near(v), pre_a, pre_b, w_out, out_b, near(bias))
    scale = math.log2(math.e) / math.sqrt(HD)
    tmp = [pltpu.VMEM((rows, 2 * local), BF)]

    part = shape((half, width), BF)
    wide_part = shape((half, width), F32)

    def pair(starts, out, name):
        ranges = [(at, half) for at in starts]
        return call(
            functools.partial(attn_pair_kernel, scale, ranges), [out] * 2, 8,
            scratch_shapes=tmp, name=name,
        )(*cache)

    sum1, sum2 = pair((3 * rows, 3 * rows + half), part, "attn_far")
    got1 = to_up(sum1)
    got2 = to_down(sum2)
    low_free, high_free = pair((rows, 2 * rows + half), part, "attn_free")
    low_free = to_down(low_free)
    high_free = to_up(high_free)
    low_need, high_need = pair((rows + half, 2 * rows), wide_part, "attn_need")
    low_need, high_need = call(add_kernel, [part] * 2, 4, name="add")(
        low_need, got2, high_need, got1
    )
    low_need = to_down(low_need)
    high_need = to_up(high_need)
    own = call(
        functools.partial(attn_own_kernel, scale, [(0, rows)]),
        shape((rows, width), F32),
        8,
        scratch_shapes=tmp,
        name="attn_own",
    )(*cache)
    own, other_w = lax.optimization_barrier((own, other_w))

    blocks = 2 * experts
    wide = blocks * SUB
    table, wm, wx, live, order = pl.pallas_call(
        functools.partial(route_kernel, zs),
        out_shape=[
            pltpu.VMEM((wide + blocks, rows), BF), pltpu.HBM((2 * rows, wide), BF),
            pltpu.HBM((2 * rows, blocks), BF), pltpu.HBM((rows, HD), F32),
            shape((experts + 1,), jnp.int32),
        ],
        in_specs=[smem(), vmem(), vmem()],
        out_specs=[vmem(), vmem(), vmem(), vmem(), smem()],
        compiler_params=limit(16),
        name="route",
    )(lengths, away(routes.T), away(route_weights.T))
    hidden, send = dispatch(
        tokens, own, high_need, low_free, high_free, low_need, moe_gain[None], near(table)
    )

    def exchange(v):
        return lax.all_to_all(v, ("x", "y", "z"), 0, 0, tiled=True)

    got = exchange(send.reshape(experts, 2 * SUB, send.shape[1]))
    back = exchange(ffn(order, got, own_w, other_w)).reshape(send.shape)
    return combine(live, back, wm, wx, hidden)


def solution(mesh):
    side = math.isqrt(mesh.shape["req"])
    grid = Mesh(
        mesh.devices.reshape(side, side, mesh.shape["exp"] // 2, 2), ("x", "y", "z", "c")
    )
    req, exp = ("x", "y"), ("z", "c")
    every = req + exp

    return jax.shard_map(
        layer,
        mesh=grid,
        in_specs=(
            P(every, None), P(), P(None, exp), P(None, exp), P(None, exp), P(exp, None),
            P(None, req, None, exp), P(), P(), P(),
            P(every, None, None), P(every, None, None), P(every, None, None),
            P(every, None), P(every, None),
        ),
        out_specs=P(every, None),
        check_vma=False,
    )
```

profile of v0, /device:TPU:24, one launch (start us, length us, event | category | flops | bytes accessed | tf_op | source)
XLA Modules:
  0.0 240.3 jit_solution(2837580359168056264)
XLA Ops:
  0.0 2.2 norm.1
  2.2 4.0 %collective-permute-start.2 = (bf16[64,2048]{1,0:T(8,128)(2,1)}, bf16[64,2048]{1,0:T(8,128)(2,1)S(1)}, u32[]{:S(2)}, u32[]{:S(2)}) collective-permute-start(bf16[64,2048]{1,0:T(8,128)(2,1)} %get-tuple-element.33), channel_id=1, source_target_pairs={{0,6},{2,0},{4,2},{6,4},{1,7},{3,1},{5,3},{7,5},{8,14},{10,8},{12,... | collective-permute-start | bytes 786440 | tf_op jit(solution)/shard_map/ppermute | solution.py:418
  6.2 3.2 %collective-permute-start.3 = (bf16[64,2048]{1,0:T(8,128)(2,1)}, bf16[64,2048]{1,0:T(8,128)(2,1)S(1)}, u32[]{:S(2)}, u32[]{:S(2)}) collective-permute-start(bf16[64,2048]{1,0:T(8,128)(2,1)} %get-tuple-element.34), channel_id=1, source_target_pairs={{0,6},{2,0},{4,2},{6,4},{1,7},{3,1},{5,3},{7,5},{8,14},{10,8},{12,... | collective-permute-start | bytes 786440 | tf_op jit(solution)/shard_map/ppermute | solution.py:418
  9.4 3.8 %collective-permute-done.2.refs_3_ = bf16[64,2048]{1,0:T(8,128)(2,1)S(1)} collective-permute-done((bf16[64,2048]{1,0:T(8,128)(2,1)}, bf16[64,2048]{1,0:T(8,128)(2,1)S(1)}, u32[]{:S(2)}, u32[]{:S(2)}) %collective-permute-start.2) | collective-permute-done | bytes 262176 | tf_op jit(solution)/shard_map/ppermute | solution.py:418
  13.2 3.6 %collective-permute-done.refs_1_ = bf16[64,2048]{1,0:T(8,128)(2,1)S(1)} collective-permute-done((bf16[64,2048]{1,0:T(8,128)(2,1)}, bf16[64,2048]{1,0:T(8,128)(2,1)S(1)}, u32[]{:S(2)}, u32[]{:S(2)}) %collective-permute-start) | collective-permute-done | bytes 262176 | tf_op jit(solution)/shard_map/ppermute | solution.py:417
  16.8 0.9 collective-permute-done.3.refs_4_
  17.7 3.3 %collective-permute-done.1.refs_2_ = bf16[64,2048]{1,0:T(8,128)(2,1)S(1)} collective-permute-done((bf16[64,2048]{1,0:T(8,128)(2,1)}, bf16[64,2048]{1,0:T(8,128)(2,1)S(1)}, u32[]{:S(2)}, u32[]{:S(2)}) %collective-permute-start.1) | collective-permute-done | bytes 262176 | tf_op jit(solution)/shard_map/ppermute | solution.py:417
  21.9 4.9 %collective-permute-done.4.refs_5_ = bf16[64,2048]{1,0:T(8,128)(2,1)} collective-permute-done((bf16[64,2048]{1,0:T(8,128)(2,1)S(1)}, bf16[64,2048]{1,0:T(8,128)(2,1)}, u32[]{:S(2)}, u32[]{:S(2)}) %collective-permute-start.4) | collective-permute-done | bytes 262176 | tf_op jit(solution)/shard_map/ppermute | solution.py:417
  27.4 2.6 %collective-permute-done.5.refs_6_ = bf16[64,2048]{1,0:T(8,128)(2,1)} collective-permute-done((bf16[64,2048]{1,0:T(8,128)(2,1)S(1)}, bf16[64,2048]{1,0:T(8,128)(2,1)}, u32[]{:S(2)}, u32[]{:S(2)}) %collective-permute-start.5) | collective-permute-done | bytes 262176 | tf_op jit(solution)/shard_map/ppermute | solution.py:418
  30.7 0.8 copy-done.12
  31.4 0.5 collective-permute-start.12
  32.0 1.1 copy.22
  33.1 1.8 prefix.1
  34.9 7.2 %all-to-all-start = ((bf16[16,64,512]{2,1,0:T(8,128)(2,1)}), bf16[16,64,512]{2,1,0:T(8,128)(2,1)S(1)}, u32[]{:S(2)}, u32[]{:S(2)}) async-start(bf16[16,64,512]{2,1,0:T(8,128)(2,1)} %bitcast.29), calls=%async_computation | async-start | bytes 2097152 | tf_op jit(solution)/shard_map/all_to_all | solution.py:449
  42.8 0.9 copy-done.11
  43.8 13.3 %all-to-all-done = bf16[16,64,512]{2,1,0:T(8,128)(2,1)S(1)} async-done(((bf16[16,64,512]{2,1,0:T(8,128)(2,1)}), bf16[16,64,512]{2,1,0:T(8,128)(2,1)S(1)}, u32[]{:S(2)}, u32[]{:S(2)}) %all-to-all-start) | async-done | bytes 1048608 | tf_op jit(solution)/shard_map/all_to_all | solution.py:449
  57.1 9.9 %qkv.1 = (bf16[512,512]{1,0:T(8,128)(2,1)S(1)}, bf16[1024,512]{1,0:T(8,128)(2,1)S(1)}, bf16[1024,512]{1,0:T(8,128)(2,1)S(1)}, f32[1,1024]{1,0:T(1,128)S(1)}) custom-call(bf16[128,2048]{1,0:T(8,128)(2,1)} %get-tuple-element.32.refs_0_, bf16[64,2048]{1,0:T(8,128)(2,1)} %copy-done.14, bf16[64,2048]{1,0:T(8,128)(2,1)} %copy-done.16, ...), custom_call_target="tpu_custom_call" | custom-call | tf_op jit(solution)/shard_map/qkv/pallas_call | solution.py:460
  67.1 2.6 %attn_far.1 = (bf16[64,2048]{1,0:T(8,128)(2,1)S(1)}, bf16[64,2048]{1,0:T(8,128)(2,1)S(1)}) custom-call(bf16[512,512]{1,0:T(8,128)(2,1)S(1)} %get-tuple-element.35.q, bf16[1024,512]{1,0:T(8,128)(2,1)S(1)} %get-tuple-element.36.k, bf16[1024,512]{1,0:T(8,128)(2,1)S(1)} %get-tuple-element.37.v, bf16[1024,512]{1,0:T(8,128)(2,1)S(1)} %bitcast.15, ...), custom_call_target="tpu_custom_call" | custom-call | tf_op jit(solution)/shard_map/attn_far/pallas_call | solution.py:492
  69.7 2.0 collective-permute-start.21
  71.8 2.6 %attn_free.1 = (bf16[64,2048]{1,0:T(8,128)(2,1)S(1)}, bf16[64,2048]{1,0:T(8,128)(2,1)S(1)}) custom-call(bf16[512,512]{1,0:T(8,128)(2,1)S(1)} %get-tuple-element.35.q, bf16[1024,512]{1,0:T(8,128)(2,1)S(1)} %get-tuple-element.36.k, bf16[1024,512]{1,0:T(8,128)(2,1)S(1)} %get-tuple-element.37.v, bf16[1024,512]{1,0:T(8,128)(2,1)S(1)} %bitcast.16, ...), custom_call_target="tpu_custom_call" | custom-call | tf_op jit(solution)/shard_map/attn_free/pallas_call | solution.py:492
  74.4 2.6 %attn_need.1 = (f32[64,2048]{1,0:T(8,128)S(1)}, f32[64,2048]{1,0:T(8,128)S(1)}) custom-call(bf16[512,512]{1,0:T(8,128)(2,1)S(1)} %get-tuple-element.35.q, bf16[1024,512]{1,0:T(8,128)(2,1)S(1)} %get-tuple-element.36.k, bf16[1024,512]{1,0:T(8,128)(2,1)S(1)} %get-tuple-element.37.v, bf16[1024,512]{1,0:T(8,128)(2,1)S(1)} %bitcast.17, ...), custom_call_target="tpu_custom_call" | custom-call | tf_op jit(solution)/shard_map/attn_need/pallas_call | solution.py:492
  77.0 1.5 collective-permute-done.21.a_got
  78.4 3.1 %collective-permute-start.24 = (bf16[64,2048]{1,0:T(8,128)(2,1)S(1)}, bf16[64,2048]{1,0:T(8,128)(2,1)S(1)}, u32[]{:S(2)}, u32[]{:S(2)}) collective-permute-start(bf16[64,2048]{1,0:T(8,128)(2,1)S(1)} %get-tuple-element.45), channel_id=1, source_target_pairs={{0,6},{2,0},{4,2},{6,4},{1,7},{3,1},{5,3},{7,5},{8,14},{10,8},{12,... | collective-permute-start | bytes 786440 | tf_op jit(solution)/shard_map/ppermute | solution.py:418
  81.8 3.3 %collective-permute-start.26 = (bf16[64,2048]{1,0:T(8,128)(2,1)S(1)}, bf16[64,2048]{1,0:T(8,128)(2,1)S(1)}, u32[]{:S(2)}, u32[]{:S(2)}) collective-permute-start(bf16[64,2048]{1,0:T(8,128)(2,1)S(1)} %get-tuple-element.47), channel_id=1, source_target_pairs={{0,6},{2,0},{4,2},{6,4},{1,7},{3,1},{5,3},{7,5},{8,14},{10,8},{12,... | collective-permute-start | bytes 786440 | tf_op jit(solution)/shard_map/ppermute | solution.py:418
  85.1 4.4 %route.1 = (bf16[1152,128]{1,0:T(8,128)(2,1)S(1)}, bf16[256,1024]{1,0:T(8,128)(2,1)}, bf16[256,128]{1,0:T(8,128)(2,1)}, f32[128,128]{1,0:T(8,128)}, s32[65]{0:T(128)S(1)}) custom-call(s32[16]{0:T(128)S(1)} %copy-done.10, s32[8,128]{1,0:T(8,128)} %bitcast.31, f32[8,128]{1,0:T(8,128)} %bitcast.32), custom_call_target="tpu_custom_call" | custom-call | tf_op jit(solution)/shard_map/route/pallas_call | solution.py:520
  89.5 2.6 %attn_own.1.own_ref = f32[128,2048]{1,0:T(8,128)S(1)} custom-call(bf16[512,512]{1,0:T(8,128)(2,1)S(1)} %get-tuple-element.35.q, bf16[1024,512]{1,0:T(8,128)(2,1)S(1)} %get-tuple-element.36.k, bf16[1024,512]{1,0:T(8,128)(2,1)S(1)} %get-tuple-element.37.v, bf16[1024,512]{1,0:T(8,128)(2,1)S(1)} %bitcast.18, bf16[1024,512]{1,0:T(8,128)(2,1)S(1)} %collective-permute-done.16.pb, ...), custom_call_target="tpu_custom_call" | custom-call | tf_op jit(solution)/shard_map/attn_own/pallas_call | solution.py:509
  92.1 3.8 %collective-permute-done.23.a1 = bf16[64,2048]{1,0:T(8,128)(2,1)S(1)} collective-permute-done((bf16[64,2048]{1,0:T(8,128)(2,1)S(1)}, bf16[64,2048]{1,0:T(8,128)(2,1)S(1)}, u32[]{:S(2)}, u32[]{:S(2)}) %collective-permute-start.23) | collective-permute-done | bytes 262176 | tf_op jit(solution)/shard_map/ppermute | solution.py:417
  96.0 1.8 dispatch.1
  97.8 61.5 %all_to_all.21.x_ref = bf16[64,16,2304]{2,1,0:T(8,128)(2,1)S(1)} all-to-all(bf16[64,16,2304]{2,1,0:T(8,128)(2,1)S(1)} %bitcast.20), channel_id=1, replica_groups=mesh['x'=4,'y'=4,'z'=4,'c'=2] {'x','y','z'}, dimensions={0} | all-to-all | bytes 9437184 | tf_op jit(solution)/shard_map/all_to_all | solution.py:537
  159.3 15.1 %ffn.1 = bf16[64,16,2304]{2,1,0:T(8,128)(2,1)S(1)} custom-call(s32[65]{0:T(128)S(1)} %get-tuple-element.31.order_ref, bf16[64,16,2304]{2,1,0:T(8,128)(2,1)S(1)} %all_to_all.21.x_ref, bf16[2048,512]{1,0:T(8,128)(2,1)S(1)} %bitcast.22, bf16[2048,512]{1,0:T(8,128)(2,1)S(1)} %bitcast.24, bf16[512,2048]{1,0:T(8,128)(2,1)S(1)} %bitcast.26, ...), custom_call_target="tpu_custom_call" | custom-call | tf_op jit(solution)/shard_map/ffn/pallas_call | solution.py:359
  174.5 63.4 %all_to_all.22 = bf16[64,16,2304]{2,1,0:T(8,128)(2,1)S(1)} all-to-all(bf16[64,16,2304]{2,1,0:T(8,128)(2,1)S(1)} %ffn.1), channel_id=1, replica_groups=mesh['x'=4,'y'=4,'z'=4,'c'=2] {'x','y','z'}, dimensions={0} | all-to-all | bytes 9437184 | tf_op jit(solution)/shard_map/all_to_all | solution.py:537
  237.9 2.4 combine.1
  (81 shorter events, 3.3 us)
Async XLA Ops:
  2.2 11.0 %collective-permute-start.2 = (bf16[64,2048]{1,0:T(8,128)(2,1)}, bf16[64,2048]{1,0:T(8,128)(2,1)S(1)}, u32[]{:S(2)}, u32[]{:S(2)}) collective-permute-start(bf16[64,2048]{1,0:T(8,128)(2,1)} %get-tuple-element.33), channel_id=1, source_target_pairs={{0,6},{2,0},{4,2},{6,4},{1,7},{3,1},{5,3},{7,5},{8,14},{10,8},{12,... | collective-permute-start | bytes 786440 | tf_op jit(solution)/shard_map/ppermute | solution.py:418
  6.2 10.6 %collective-permute-start = (bf16[64,2048]{1,0:T(8,128)(2,1)}, bf16[64,2048]{1,0:T(8,128)(2,1)S(1)}, u32[]{:S(2)}, u32[]{:S(2)}) collective-permute-start(bf16[64,2048]{1,0:T(8,128)(2,1)} %get-tuple-element.33), channel_id=1, source_target_pairs={{0,2},{2,4},{4,6},{6,0},{1,3},{3,5},{5,7},{7,1},{8,10},{10,12},{12... | collective-permute-start | bytes 786440 | tf_op jit(solution)/shard_map/ppermute | solution.py:417
  6.2 11.5 %collective-permute-start.3 = (bf16[64,2048]{1,0:T(8,128)(2,1)}, bf16[64,2048]{1,0:T(8,128)(2,1)S(1)}, u32[]{:S(2)}, u32[]{:S(2)}) collective-permute-start(bf16[64,2048]{1,0:T(8,128)(2,1)} %get-tuple-element.34), channel_id=1, source_target_pairs={{0,6},{2,0},{4,2},{6,4},{1,7},{3,1},{5,3},{7,5},{8,14},{10,8},{12,... | collective-permute-start | bytes 786440 | tf_op jit(solution)/shard_map/ppermute | solution.py:418
  9.4 11.6 %collective-permute-start.1 = (bf16[64,2048]{1,0:T(8,128)(2,1)}, bf16[64,2048]{1,0:T(8,128)(2,1)S(1)}, u32[]{:S(2)}, u32[]{:S(2)}) collective-permute-start(bf16[64,2048]{1,0:T(8,128)(2,1)} %get-tuple-element.34), channel_id=1, source_target_pairs={{0,2},{2,4},{4,6},{6,0},{1,3},{3,5},{5,7},{7,1},{8,10},{10,12},{12... | collective-permute-start | bytes 786440 | tf_op jit(solution)/shard_map/ppermute | solution.py:417
  13.2 7.8 %collective-permute-start.9 = (bf16[64,2048]{1,0:T(8,128)(2,1)S(1)}, bf16[64,2048]{1,0:T(8,128)(2,1)S(1)}, u32[]{:S(2)}, u32[]{:S(2)}) collective-permute-start(bf16[64,2048]{1,0:T(8,128)(2,1)S(1)} %collective-permute-done.2.refs_3_), channel_id=1, source_target_pairs={{0,1},{1,0},{2,3},{3,2},{4,5},{5,4},{6,7},{7,6},{8,9},{9,8},{10,11... | collective-permute-start | bytes 786440 | tf_op jit(solution)/shard_map/ppermute | solution.py:416
  16.8 4.7 %collective-permute-start.7 = (bf16[64,2048]{1,0:T(8,128)(2,1)S(1)}, bf16[64,2048]{1,0:T(8,128)(2,1)S(1)}, u32[]{:S(2)}, u32[]{:S(2)}) collective-permute-start(bf16[64,2048]{1,0:T(8,128)(2,1)S(1)} %collective-permute-done.refs_1_), channel_id=1, source_target_pairs={{0,1},{1,0},{2,3},{3,2},{4,5},{5,4},{6,7},{7,6},{8,9},{9,8},{10,11... | collective-permute-start | bytes 786440 | tf_op jit(solution)/shard_map/ppermute | solution.py:416
  16.8 10.0 %collective-permute-start.4 = (bf16[64,2048]{1,0:T(8,128)(2,1)S(1)}, bf16[64,2048]{1,0:T(8,128)(2,1)}, u32[]{:S(2)}, u32[]{:S(2)}) collective-permute-start(bf16[64,2048]{1,0:T(8,128)(2,1)S(1)} %collective-permute-done.refs_1_), channel_id=1, source_target_pairs={{0,2},{2,4},{4,6},{6,0},{1,3},{3,5},{5,7},{7,1},{8,10},{10,12},{12... | collective-permute-start | bytes 786440 | tf_op jit(solution)/shard_map/ppermute | solution.py:417
  17.7 25.0 %collective-permute-start.14 = (bf16[2048,256]{1,0:T(8,128)(2,1)}, bf16[2048,256]{1,0:T(8,128)(2,1)S(1)}, u32[]{:S(2)}, u32[]{:S(2)}) collective-permute-start(bf16[2048,256]{1,0:T(8,128)(2,1)} %refs_16_.1), channel_id=1, source_target_pairs={{0,1},{1,0},{2,3},{3,2},{4,5},{5,4},{6,7},{7,6},{8,9},{9,8},{10,11... | collective-permute-start | bytes 3145736 | tf_op jit(solution)/shard_map/ppermute | solution.py:416
  21.0 9.5 %collective-permute-start.6 = (bf16[128,2048]{1,0:T(8,128)(2,1)}, bf16[128,2048]{1,0:T(8,128)(2,1)S(1)}, u32[]{:S(2)}, u32[]{:S(2)}) collective-permute-start(bf16[128,2048]{1,0:T(8,128)(2,1)} %get-tuple-element.32.refs_0_), channel_id=1, source_target_pairs={{0,1},{1,0},{2,3},{3,2},{4,5},{5,4},{6,7},{7,6},{8,9},{9,8},{10,11... | collective-permute-start | bytes 1572872 | tf_op jit(solution)/shard_map/ppermute | solution.py:416
  21.0 5.8 %collective-permute-start.10 = (bf16[64,2048]{1,0:T(8,128)(2,1)S(1)}, bf16[64,2048]{1,0:T(8,128)(2,1)S(1)}, u32[]{:S(2)}, u32[]{:S(2)}) collective-permute-start(bf16[64,2048]{1,0:T(8,128)(2,1)S(1)} %collective-permute-done.3.refs_4_), channel_id=1, source_target_pairs={{0,1},{1,0},{2,3},{3,2},{4,5},{5,4},{6,7},{7,6},{8,9},{9,8},{10,11... | collective-permute-start | bytes 786440 | tf_op jit(solution)/shard_map/ppermute | solution.py:416
  21.5 8.4 %collective-permute-start.5 = (bf16[64,2048]{1,0:T(8,128)(2,1)S(1)}, bf16[64,2048]{1,0:T(8,128)(2,1)}, u32[]{:S(2)}, u32[]{:S(2)}) collective-permute-start(bf16[64,2048]{1,0:T(8,128)(2,1)S(1)} %collective-permute-done.3.refs_4_), channel_id=1, source_target_pairs={{0,6},{2,0},{4,2},{6,4},{1,7},{3,1},{5,3},{7,5},{8,14},{10,8},{12,... | collective-permute-start | bytes 786440 | tf_op jit(solution)/shard_map/ppermute | solution.py:418
  26.8 3.1 %collective-permute-start.8 = (bf16[64,2048]{1,0:T(8,128)(2,1)S(1)}, bf16[64,2048]{1,0:T(8,128)(2,1)S(1)}, u32[]{:S(2)}, u32[]{:S(2)}) collective-permute-start(bf16[64,2048]{1,0:T(8,128)(2,1)S(1)} %collective-permute-done.1.refs_2_), channel_id=1, source_target_pairs={{0,1},{1,0},{2,3},{3,2},{4,5},{5,4},{6,7},{7,6},{8,9},{9,8},{10,11... | collective-permute-start | bytes 786440 | tf_op jit(solution)/shard_map/ppermute | solution.py:416
  26.8 16.8 %collective-permute-start.13 = (bf16[2048,256]{1,0:T(8,128)(2,1)}, bf16[2048,256]{1,0:T(8,128)(2,1)}, u32[]{:S(2)}, u32[]{:S(2)}) collective-permute-start(bf16[2048,256]{1,0:T(8,128)(2,1)} %refs_14_.1), channel_id=1, source_target_pairs={{0,1},{1,0},{2,3},{3,2},{4,5},{5,4},{6,7},{7,6},{8,9},{9,8},{10,11... | collective-permute-start | bytes 3145736 | tf_op jit(solution)/shard_map/ppermute | solution.py:416
  29.9 27.2 %collective-permute-start.15 = (bf16[2048,256]{1,0:T(8,128)(2,1)}, bf16[2048,256]{1,0:T(8,128)(2,1)}, u32[]{:S(2)}, u32[]{:S(2)}) collective-permute-start(bf16[2048,256]{1,0:T(8,128)(2,1)} %refs_18_.1), channel_id=1, source_target_pairs={{0,1},{1,0},{2,3},{3,2},{4,5},{5,4},{6,7},{7,6},{8,9},{9,8},{10,11... | collective-permute-start | bytes 3145736 | tf_op jit(solution)/shard_map/ppermute | solution.py:416
  29.9 12.1 %collective-permute-start.11 = (bf16[64,2048]{1,0:T(8,128)(2,1)}, bf16[64,2048]{1,0:T(8,128)(2,1)}, u32[]{:S(2)}, u32[]{:S(2)}) collective-permute-start(bf16[64,2048]{1,0:T(8,128)(2,1)} %collective-permute-done.4.refs_5_), channel_id=1, source_target_pairs={{0,1},{1,0},{2,3},{3,2},{4,5},{5,4},{6,7},{7,6},{8,9},{9,8},{10,11... | collective-permute-start | bytes 786440 | tf_op jit(solution)/shard_map/ppermute | solution.py:416
  31.4 10.8 %collective-permute-start.12 = (bf16[64,2048]{1,0:T(8,128)(2,1)}, bf16[64,2048]{1,0:T(8,128)(2,1)}, u32[]{:S(2)}, u32[]{:S(2)}) collective-permute-start(bf16[64,2048]{1,0:T(8,128)(2,1)} %collective-permute-done.5.refs_6_), channel_id=1, source_target_pairs={{0,1},{1,0},{2,3},{3,2},{4,5},{5,4},{6,7},{7,6},{8,9},{9,8},{10,11... | collective-permute-start | bytes 786440 | tf_op jit(solution)/shard_map/ppermute | solution.py:416
  34.9 22.2 %all-to-all-start = ((bf16[16,64,512]{2,1,0:T(8,128)(2,1)}), bf16[16,64,512]{2,1,0:T(8,128)(2,1)S(1)}, u32[]{:S(2)}, u32[]{:S(2)}) async-start(bf16[16,64,512]{2,1,0:T(8,128)(2,1)} %bitcast.29), calls=%async_computation | async-start | bytes 2097152 | tf_op jit(solution)/shard_map/all_to_all | solution.py:449
  42.1 39.6 %collective-permute-start.18 = (bf16[2048,512]{1,0:T(8,128)(2,1)}, bf16[2048,512]{1,0:T(8,128)(2,1)}, u32[]{:S(2)}, u32[]{:S(2)}) collective-permute-start(bf16[2048,512]{1,0:T(8,128)(2,1)} %bitcast.21), channel_id=1, source_target_pairs={{0,1},{1,0},{2,3},{3,2},{4,5},{5,4},{6,7},{7,6},{8,9},{9,8},{10,11... | collective-permute-start | bytes 6291464 | tf_op jit(solution)/shard_map/ppermute | solution.py:416
  42.2 39.6 %collective-permute-start.19 = (bf16[2048,512]{1,0:T(8,128)(2,1)}, bf16[2048,512]{1,0:T(8,128)(2,1)}, u32[]{:S(2)}, u32[]{:S(2)}) collective-permute-start(bf16[2048,512]{1,0:T(8,128)(2,1)} %bitcast.23), channel_id=1, source_target_pairs={{0,1},{1,0},{2,3},{3,2},{4,5},{5,4},{6,7},{7,6},{8,9},{9,8},{10,11... | collective-permute-start | bytes 6291464 | tf_op jit(solution)/shard_map/ppermute | solution.py:416
  42.7 49.4 %collective-permute-start.20 = (bf16[512,2048]{1,0:T(8,128)(2,1)}, bf16[512,2048]{1,0:T(8,128)(2,1)}, u32[]{:S(2)}, u32[]{:S(2)}) collective-permute-start(bf16[512,2048]{1,0:T(8,128)(2,1)} %bitcast.25), channel_id=1, source_target_pairs={{0,1},{1,0},{2,3},{3,2},{4,5},{5,4},{6,7},{7,6},{8,9},{9,8},{10,11... | collective-permute-start | bytes 6291464 | tf_op jit(solution)/shard_map/ppermute | solution.py:416
  43.7 23.4 %collective-permute-start.17 = (bf16[256,2048]{1,0:T(8,128)(2,1)S(1)}, bf16[256,2048]{1,0:T(8,128)(2,1)S(1)}, u32[]{:S(2)}, u32[]{:S(2)}) collective-permute-start(bf16[256,2048]{1,0:T(8,128)(2,1)S(1)} %copy-done), channel_id=1, source_target_pairs={{0,1},{1,0},{2,3},{3,2},{4,5},{5,4},{6,7},{7,6},{8,9},{9,8},{10,11... | collective-permute-start | bytes 3145736 | tf_op jit(solution)/shard_map/ppermute | solution.py:416
  57.1 10.0 %collective-permute-start.16 = (bf16[1024,512]{1,0:T(8,128)(2,1)S(1)}, bf16[1024,512]{1,0:T(8,128)(2,1)S(1)}, u32[]{:S(2)}, u32[]{:S(2)}) collective-permute-start(bf16[1024,512]{1,0:T(8,128)(2,1)S(1)} %bitcast.14), channel_id=1, source_target_pairs={{0,1},{1,0},{2,3},{3,2},{4,5},{5,4},{6,7},{7,6},{8,9},{9,8},{10,11... | collective-permute-start | bytes 3145736 | tf_op jit(solution)/shard_map/ppermute | solution.py:416
  69.7 8.8 %collective-permute-start.21 = (bf16[64,2048]{1,0:T(8,128)(2,1)S(1)}, bf16[64,2048]{1,0:T(8,128)(2,1)S(1)}, u32[]{:S(2)}, u32[]{:S(2)}) collective-permute-start(bf16[64,2048]{1,0:T(8,128)(2,1)S(1)} %get-tuple-element.41), channel_id=1, source_target_pairs={{0,6},{2,0},{4,2},{6,4},{1,7},{3,1},{5,3},{7,5},{8,14},{10,8},{12,... | collective-permute-start | bytes 786440 | tf_op jit(solution)/shard_map/ppermute | solution.py:418
  71.7 9.9 %collective-permute-start.22 = (bf16[64,2048]{1,0:T(8,128)(2,1)S(1)}, bf16[64,2048]{1,0:T(8,128)(2,1)S(1)}, u32[]{:S(2)}, u32[]{:S(2)}) collective-permute-start(bf16[64,2048]{1,0:T(8,128)(2,1)S(1)} %get-tuple-element.43), channel_id=1, source_target_pairs={{0,2},{2,4},{4,6},{6,0},{1,3},{3,5},{5,7},{7,1},{8,10},{10,12},{12... | collective-permute-start | bytes 786440 | tf_op jit(solution)/shard_map/ppermute | solution.py:417
  78.4 13.7 %collective-permute-start.24 = (bf16[64,2048]{1,0:T(8,128)(2,1)S(1)}, bf16[64,2048]{1,0:T(8,128)(2,1)S(1)}, u32[]{:S(2)}, u32[]{:S(2)}) collective-permute-start(bf16[64,2048]{1,0:T(8,128)(2,1)S(1)} %get-tuple-element.45), channel_id=1, source_target_pairs={{0,6},{2,0},{4,2},{6,4},{1,7},{3,1},{5,3},{7,5},{8,14},{10,8},{12,... | collective-permute-start | bytes 786440 | tf_op jit(solution)/shard_map/ppermute | solution.py:418
  81.6 10.5 %collective-permute-start.25 = (bf16[64,2048]{1,0:T(8,128)(2,1)S(1)}, bf16[64,2048]{1,0:T(8,128)(2,1)S(1)}, u32[]{:S(2)}, u32[]{:S(2)}) collective-permute-start(bf16[64,2048]{1,0:T(8,128)(2,1)S(1)} %get-tuple-element.46), channel_id=1, source_target_pairs={{0,2},{2,4},{4,6},{6,0},{1,3},{3,5},{5,7},{7,1},{8,10},{10,12},{12... | collective-permute-start | bytes 786440 | tf_op jit(solution)/shard_map/ppermute | solution.py:417
  81.7 14.3 %collective-permute-start.23 = (bf16[64,2048]{1,0:T(8,128)(2,1)S(1)}, bf16[64,2048]{1,0:T(8,128)(2,1)S(1)}, u32[]{:S(2)}, u32[]{:S(2)}) collective-permute-start(bf16[64,2048]{1,0:T(8,128)(2,1)S(1)} %get-tuple-element.44), channel_id=1, source_target_pairs={{0,2},{2,4},{4,6},{6,0},{1,3},{3,5},{5,7},{7,1},{8,10},{10,12},{12... | collective-permute-start | bytes 786440 | tf_op jit(solution)/shard_map/ppermute | solution.py:417
  81.8 14.2 %collective-permute-start.26 = (bf16[64,2048]{1,0:T(8,128)(2,1)S(1)}, bf16[64,2048]{1,0:T(8,128)(2,1)S(1)}, u32[]{:S(2)}, u32[]{:S(2)}) collective-permute-start(bf16[64,2048]{1,0:T(8,128)(2,1)S(1)} %get-tuple-element.47), channel_id=1, source_target_pairs={{0,6},{2,0},{4,2},{6,4},{1,7},{3,1},{5,3},{7,5},{8,14},{10,8},{12,... | collective-permute-start | bytes 786440 | tf_op jit(solution)/shard_map/ppermute | solution.py:418
  174.4 63.4 %copy-start.5 = (bf16[256,1024]{1,0:T(8,128)(2,1)S(1)}, bf16[256,1024]{1,0:T(8,128)(2,1)}, u32[]{:S(2)}) copy-start(bf16[256,1024]{1,0:T(8,128)(2,1)} %get-tuple-element.53.wm_ref) | copy-start | bytes 1572868
  174.4 63.4 %copy-start.6 = (bf16[128,2048]{1,0:T(8,128)(2,1)S(1)}, bf16[128,2048]{1,0:T(8,128)(2,1)}, u32[]{:S(2)}) copy-start(bf16[128,2048]{1,0:T(8,128)(2,1)} %get-tuple-element.55.h_ref) | copy-start | bytes 1572868
  174.5 63.4 %copy-start.7 = (bf16[256,128]{1,0:T(8,128)(2,1)S(1)}, bf16[256,128]{1,0:T(8,128)(2,1)}, u32[]{:S(2)}) copy-start(bf16[256,128]{1,0:T(8,128)(2,1)} %get-tuple-element.54.wx_ref) | copy-start | bytes 196612
  174.5 63.4 %copy-start.8 = (f32[128,128]{1,0:T(8,128)S(1)}, f32[128,128]{1,0:T(8,128)}, u32[]{:S(2)}) copy-start(f32[128,128]{1,0:T(8,128)} %get-tuple-element.56.live_ref) | copy-start | bytes 196612
  (17 other events, 323.2 us)
where the time goes:
time: 243 us; the launch traced here: 240 us
  blocking collectives  125 us (51%)
  Pallas kernels  48.1 us (20%)
  waiting for transfers between devices  37.7 us (16%)
  starting transfers between devices  26.2 us (11%)
  local copies, waits for them, and re-layouts  3.01 us (1%)
    all_to_all x2, blocking collectives, exchange(): return lax.all_to_all(v, ('x', 'y', 'z'), 0, 0, tiled=True)  125 us
    ppermute x6, starting transfers between devices, layer(): to_down = lambda v: lax.ppermute(v, 'z', down)  16.1 us
    ppermute x6, waiting for transfers between devices, layer(): to_up = lambda v: lax.ppermute(v, 'z', up)  15.7 us
    pallas_call x1, Pallas kernels, ffn(): pl.pallas_call(functools.partial(ffn_kernel, group), out_shape=pltpu.VMEM...  15.1 us
    all_to_all x1, waiting for transfers between devices, layer(): lax.all_to_all(outgoing, ('x', 'y'), split_axis=0, concat_axis=0, tiled=T...  13.3 us
    pallas_call x1, Pallas kernels, layer(): pl.pallas_call(lambda *refs: qkv_kernel(len(pieces), *refs), out_shape=(p...  9.95 us
    ppermute x6, waiting for transfers between devices, layer(): to_down = lambda v: lax.ppermute(v, 'z', down)  8.72 us
    pallas_call x3, Pallas kernels, pair(): call(functools.partial(attn_pair_kernel, scale, ranges), [out] * 2, 8, sc...  7.77 us
  transfers between devices with their start and end apart: 28, of which 9 were waited for; matrix products, arithmetic and copies ran while one was open for 0% of the time, Pallas kernels for 11%

commit v1 on v0

--- a/solution.py
+++ b/solution.py
@@ -182,9 +182,12 @@
         )
         for i, w in enumerate(weights)
     ]
-    early = len(copies) // 2
-    for copy in (*loads[:2], *copies[:early], *loads[2:], *copies[early:]):
+    for load in loads[:2]:
+        load.start()
+    for copy in copies:
         copy.start()
+    for load in loads[2:]:
+        load.start()
     facts = pltpu.make_async_copy(len_hbm, len_ref, len_sem)
     facts.start()
     n = c1_ref.shape[0]
@@ -221,14 +224,15 @@
                 o_ref[rows, h * HD : (h + 1) * HD] = turned.astype(BF)
 
 
-def attend(scale, q_ref, k_ref, v_ref, pre_refs, bias_ref, o_ref, ranges):
+def attend(scale, q_ref, k_ref, v_ref, pre_refs, bias_ref, o_ref, first):
     local = pre_refs[0].shape[1] // 2
+    rows = o_ref.shape[0]
     nt = (((1,), (1,)), ((), ()))
     for h in range(q_ref.shape[1] // HD):
         side, col = divmod(h * HD, local)
         pre_ref = pre_refs[side]
         cols = slice(h * HD, (h + 1) * HD)
-        q = jnp.concatenate([q_ref[at : at + n, cols] for at, n in ranges], axis=0)
+        q = q_ref[first : first + rows, cols]
         s1 = lax.dot_general(q, pre_ref[:, col : col + HD], nt, preferred_element_type=F32)
         s2 = lax.dot_general(q, k_ref[:, cols], nt, preferred_element_type=F32) + bias_ref[...]
         top = jnp.maximum(
@@ -247,16 +251,27 @@
     return dot(a_ref[:, :local], wa_ref[...]) + dot(a_ref[:, local:], wb_ref[...])
 
 
-def attn_pair_kernel(scale, ranges, q, k, v, pa, pb, wa, wb, bias, o1, o2, tmp):
-    attend(scale, q, k, v, (pa, pb), bias, tmp, ranges)
+def attn_far_kernel(scale, first, q, k, v, pa, pb, wa, wb, bias, o1, o2, tmp):
+    attend(scale, q, k, v, (pa, pb), bias, tmp, first)
+    total = project(tmp, wa, wb).astype(BF)
+    rows = o1.shape[0]
+    o1[...] = total[:rows]
+    o2[...] = total[rows:]
+
+
+def attn_near_kernel(
+    scale, first, q, k, v, pa, pb, wa, wb, bias, low_free, low_need, high_need, high_free,
+    tmp,
+):
+    attend(scale, q, k, v, (pa, pb), bias, tmp, first)
     total = project(tmp, wa, wb)
-    rows = o1.shape[0]
-    o1[...] = total[:rows].astype(o1.dtype)
-    o2[...] = total[rows:].astype(o2.dtype)
-
-
-def attn_own_kernel(scale, ranges, q, k, v, pa, pb, wa, wb, bias, o, tmp):
-    attend(scale, q, k, v, (pa, pb), bias, tmp, ranges)
+    n = low_free.shape[0]
+    for i, o_ref in enumerate((low_free, low_need, high_need, high_free)):
+        o_ref[...] = total[i * n : (i + 1) * n].astype(o_ref.dtype)
+
+
+def attn_own_kernel(scale, first, q, k, v, pa, pb, wa, wb, bias, o, tmp):
+    attend(scale, q, k, v, (pa, pb), bias, tmp, first)
     o[...] = project(tmp, wa, wb)
 
 
@@ -452,6 +467,7 @@
     own_w = (w_gate[0], w_up[0], w_down[0])
     other_w = tuple(swap(w) for w in own_w)
 
+    far0, far1 = lax.optimization_barrier((far0, far1))
     far_b = swap(far0), swap(far1)
 
 
@@ -484,30 +500,33 @@
     scale = math.log2(math.e) / math.sqrt(HD)
     tmp = [pltpu.VMEM((rows, 2 * local), BF)]
 
+    sum1, sum2 = call(
+        functools.partial(attn_far_kernel, scale, 3 * rows),
+        [shape((half, width), BF)] * 2,
+        8,
+        scratch_shapes=tmp,
+        name="attn_far",
+    )(*cache)
+    got1 = to_up(sum1)
+    got2 = to_down(sum2)
     part = shape((half, width), BF)
     wide_part = shape((half, width), F32)
-
-    def pair(starts, out, name):
-        ranges = [(at, half) for at in starts]
-        return call(
-            functools.partial(attn_pair_kernel, scale, ranges), [out] * 2, 8,
-            scratch_shapes=tmp, name=name,
-        )(*cache)
-
-    sum1, sum2 = pair((3 * rows, 3 * rows + half), part, "attn_far")
-    got1 = to_up(sum1)
-    got2 = to_down(sum2)
-    low_free, high_free = pair((rows, 2 * rows + half), part, "attn_free")
+    low_free, low_need, high_need, high_free = call(
+        functools.partial(attn_near_kernel, scale, rows),
+        [part, wide_part, wide_part, part],
+        8,
+        scratch_shapes=[pltpu.VMEM((2 * rows, 2 * local), BF)],
+        name="attn_near",
+    )(*cache)
     low_free = to_down(low_free)
     high_free = to_up(high_free)
-    low_need, high_need = pair((rows + half, 2 * rows), wide_part, "attn_need")
     low_need, high_need = call(add_kernel, [part] * 2, 4, name="add")(
         low_need, got2, high_need, got1
     )
     low_need = to_down(low_need)
     high_need = to_up(high_need)
     own = call(
-        functools.partial(attn_own_kernel, scale, [(0, rows)]),
+        functools.partial(attn_own_kernel, scale, 0),
         shape((rows, width), F32),
         8,
         scratch_shapes=tmp,

time: 243 us -> 243 us (level)
    pallas_call x4 -> x3, Pallas kernels: 10.4 us -> 9.29 us  [the longest x1 4.1 us: layer(): call(functools.partial(attn_near_kernel, scale, rows), [part, wide_part,...]
where the time goes in v1:
time: 243 us; the launch traced here: 240 us
  blocking collectives  125 us (51%)
  Pallas kernels  47 us (19%)
  waiting for transfers between devices  38.6 us (16%)
  starting transfers between devices  26.5 us (11%)
  local copies, waits for them, and re-layouts  2.99 us (1%)
    all_to_all x2, blocking collectives, exchange(): return lax.all_to_all(v, ('x', 'y', 'z'), 0, 0, tiled=True)  125 us
    ppermute x6, starting transfers between devices, layer(): to_down = lambda v: lax.ppermute(v, 'z', down)  16.1 us
    ppermute x6, waiting for transfers between devices, layer(): to_up = lambda v: lax.ppermute(v, 'z', up)  15.4 us
    pallas_call x1, Pallas kernels, ffn(): pl.pallas_call(functools.partial(ffn_kernel, group), out_shape=pltpu.VMEM...  15.1 us
    all_to_all x1, waiting for transfers between devices, layer(): lax.all_to_all(outgoing, ('x', 'y'), split_axis=0, concat_axis=0, tiled=T...  13.3 us
    pallas_call x1, Pallas kernels, layer(): pl.pallas_call(lambda *refs: qkv_kernel(len(pieces), *refs), out_shape=(p...  9.94 us
    ppermute x6, waiting for transfers between devices, layer(): to_down = lambda v: lax.ppermute(v, 'z', down)  9.81 us
    all_to_all x1, starting transfers between devices, layer(): lax.all_to_all(outgoing, ('x', 'y'), split_axis=0, concat_axis=0, tiled=T...  7.17 us
  transfers between devices with their start and end apart: 28, of which 9 were waited for; matrix products, arithmetic and copies ran while one was open for 0% of the time, Pallas kernels for 11%

profile of v1, /device:TPU:24, one launch (start us, length us, event | category | flops | bytes accessed | tf_op | source)
XLA Modules:
  0.0 240.3 jit_solution(7115059018463988039)
XLA Ops:
  0.0 2.2 norm.1
  2.2 4.0 %collective-permute-start.2 = (bf16[64,2048]{1,0:T(8,128)(2,1)}, bf16[64,2048]{1,0:T(8,128)(2,1)S(1)}, u32[]{:S(2)}, u32[]{:S(2)}) collective-permute-start(bf16[64,2048]{1,0:T(8,128)(2,1)} %get-tuple-element.35), channel_id=1, source_target_pairs={{0,6},{2,0},{4,2},{6,4},{1,7},{3,1},{5,3},{7,5},{8,14},{10,8},{12,... | collective-permute-start | bytes 786440 | tf_op jit(solution)/shard_map/ppermute | solution.py:433
  6.2 3.2 %collective-permute-start.3 = (bf16[64,2048]{1,0:T(8,128)(2,1)}, bf16[64,2048]{1,0:T(8,128)(2,1)S(1)}, u32[]{:S(2)}, u32[]{:S(2)}) collective-permute-start(bf16[64,2048]{1,0:T(8,128)(2,1)} %get-tuple-element.36), channel_id=1, source_target_pairs={{0,6},{2,0},{4,2},{6,4},{1,7},{3,1},{5,3},{7,5},{8,14},{10,8},{12,... | collective-permute-start | bytes 786440 | tf_op jit(solution)/shard_map/ppermute | solution.py:433
  9.4 3.8 %collective-permute-done.2.refs_3_ = bf16[64,2048]{1,0:T(8,128)(2,1)S(1)} collective-permute-done((bf16[64,2048]{1,0:T(8,128)(2,1)}, bf16[64,2048]{1,0:T(8,128)(2,1)S(1)}, u32[]{:S(2)}, u32[]{:S(2)}) %collective-permute-start.2) | collective-permute-done | bytes 262176 | tf_op jit(solution)/shard_map/ppermute | solution.py:433
  13.2 3.6 %collective-permute-done.refs_1_ = bf16[64,2048]{1,0:T(8,128)(2,1)S(1)} collective-permute-done((bf16[64,2048]{1,0:T(8,128)(2,1)}, bf16[64,2048]{1,0:T(8,128)(2,1)S(1)}, u32[]{:S(2)}, u32[]{:S(2)}) %collective-permute-start) | collective-permute-done | bytes 262176 | tf_op jit(solution)/shard_map/ppermute | solution.py:432
  16.8 0.9 collective-permute-done.3.refs_4_
  17.7 3.3 %collective-permute-done.1.refs_2_ = bf16[64,2048]{1,0:T(8,128)(2,1)S(1)} collective-permute-done((bf16[64,2048]{1,0:T(8,128)(2,1)}, bf16[64,2048]{1,0:T(8,128)(2,1)S(1)}, u32[]{:S(2)}, u32[]{:S(2)}) %collective-permute-start.1) | collective-permute-done | bytes 262176 | tf_op jit(solution)/shard_map/ppermute | solution.py:432
  21.9 4.9 %collective-permute-done.4.refs_5_ = bf16[64,2048]{1,0:T(8,128)(2,1)} collective-permute-done((bf16[64,2048]{1,0:T(8,128)(2,1)S(1)}, bf16[64,2048]{1,0:T(8,128)(2,1)}, u32[]{:S(2)}, u32[]{:S(2)}) %collective-permute-start.4) | collective-permute-done | bytes 262176 | tf_op jit(solution)/shard_map/ppermute | solution.py:432
  26.9 0.5 collective-permute-start.13
  27.4 2.6 %collective-permute-done.5.refs_6_ = bf16[64,2048]{1,0:T(8,128)(2,1)} collective-permute-done((bf16[64,2048]{1,0:T(8,128)(2,1)S(1)}, bf16[64,2048]{1,0:T(8,128)(2,1)}, u32[]{:S(2)}, u32[]{:S(2)}) %collective-permute-start.5) | collective-permute-done | bytes 262176 | tf_op jit(solution)/shard_map/ppermute | solution.py:433
  30.7 0.8 copy-done.12
  31.4 0.5 collective-permute-start.12
  32.0 1.1 copy.22
  33.1 1.8 prefix.1
  34.9 7.2 %all-to-all-start = ((bf16[16,64,512]{2,1,0:T(8,128)(2,1)}), bf16[16,64,512]{2,1,0:T(8,128)(2,1)S(1)}, u32[]{:S(2)}, u32[]{:S(2)}) async-start(bf16[16,64,512]{2,1,0:T(8,128)(2,1)} %bitcast.28), calls=%async_computation | async-start | bytes 2097152 | tf_op jit(solution)/shard_map/all_to_all | solution.py:464
  42.8 0.9 copy-done.11
  43.8 13.3 %all-to-all-done = bf16[16,64,512]{2,1,0:T(8,128)(2,1)S(1)} async-done(((bf16[16,64,512]{2,1,0:T(8,128)(2,1)}), bf16[16,64,512]{2,1,0:T(8,128)(2,1)S(1)}, u32[]{:S(2)}, u32[]{:S(2)}) %all-to-all-start) | async-done | bytes 1048608 | tf_op jit(solution)/shard_map/all_to_all | solution.py:464
  57.1 9.9 %qkv.1 = (bf16[512,512]{1,0:T(8,128)(2,1)S(1)}, bf16[1024,512]{1,0:T(8,128)(2,1)S(1)}, bf16[1024,512]{1,0:T(8,128)(2,1)S(1)}, f32[1,1024]{1,0:T(1,128)S(1)}) custom-call(bf16[128,2048]{1,0:T(8,128)(2,1)} %get-tuple-element.34.refs_0_, bf16[64,2048]{1,0:T(8,128)(2,1)} %copy-done.14, bf16[64,2048]{1,0:T(8,128)(2,1)} %copy-done.16, ...), custom_call_target="tpu_custom_call" | custom-call | tf_op jit(solution)/shard_map/qkv/pallas_call | solution.py:476
  67.1 2.6 %attn_far.1 = (bf16[64,2048]{1,0:T(8,128)(2,1)S(1)}, bf16[64,2048]{1,0:T(8,128)(2,1)S(1)}) custom-call(bf16[512,512]{1,0:T(8,128)(2,1)S(1)} %get-tuple-element.39.q, bf16[1024,512]{1,0:T(8,128)(2,1)S(1)} %get-tuple-element.40.k, bf16[1024,512]{1,0:T(8,128)(2,1)S(1)} %get-tuple-element.41.v, bf16[1024,512]{1,0:T(8,128)(2,1)S(1)} %bitcast.16, ...), custom_call_target="tpu_custom_call" | custom-call | tf_op jit(solution)/shard_map/attn_far/pallas_call | solution.py:503
  69.7 2.0 collective-permute-start.21
  71.8 4.1 %attn_near.1 = (bf16[64,2048]{1,0:T(8,128)(2,1)S(1)}, f32[64,2048]{1,0:T(8,128)S(1)}, f32[64,2048]{1,0:T(8,128)S(1)}, bf16[64,2048]{1,0:T(8,128)(2,1)S(1)}) custom-call(bf16[512,512]{1,0:T(8,128)(2,1)S(1)} %get-tuple-element.39.q, bf16[1024,512]{1,0:T(8,128)(2,1)S(1)} %get-tuple-element.40.k, bf16[1024,512]{1,0:T(8,128)(2,1)S(1)} %get-tuple-element.41.v, ...), custom_call_target="tpu_custom_call" | custom-call | tf_op jit(solution)/shard_map/attn_near/pallas_call | solution.py:514
  75.9 2.6 %collective-permute-done.21.a_got = bf16[64,2048]{1,0:T(8,128)(2,1)S(1)} collective-permute-done((bf16[64,2048]{1,0:T(8,128)(2,1)S(1)}, bf16[64,2048]{1,0:T(8,128)(2,1)S(1)}, u32[]{:S(2)}, u32[]{:S(2)}) %collective-permute-start.21) | collective-permute-done | bytes 262176 | tf_op jit(solution)/shard_map/ppermute | solution.py:433
  78.4 3.1 %collective-permute-start.24 = (bf16[64,2048]{1,0:T(8,128)(2,1)S(1)}, bf16[64,2048]{1,0:T(8,128)(2,1)S(1)}, u32[]{:S(2)}, u32[]{:S(2)}) collective-permute-start(bf16[64,2048]{1,0:T(8,128)(2,1)S(1)} %get-tuple-element.49), channel_id=1, source_target_pairs={{0,6},{2,0},{4,2},{6,4},{1,7},{3,1},{5,3},{7,5},{8,14},{10,8},{12,... | collective-permute-start | bytes 786440 | tf_op jit(solution)/shard_map/ppermute | solution.py:433
  82.0 3.3 %collective-permute-start.26 = (bf16[64,2048]{1,0:T(8,128)(2,1)S(1)}, bf16[64,2048]{1,0:T(8,128)(2,1)S(1)}, u32[]{:S(2)}, u32[]{:S(2)}) collective-permute-start(bf16[64,2048]{1,0:T(8,128)(2,1)S(1)} %get-tuple-element.51), channel_id=1, source_target_pairs={{0,6},{2,0},{4,2},{6,4},{1,7},{3,1},{5,3},{7,5},{8,14},{10,8},{12,... | collective-permute-start | bytes 786440 | tf_op jit(solution)/shard_map/ppermute | solution.py:433
  85.3 4.4 %route.1 = (bf16[1152,128]{1,0:T(8,128)(2,1)S(1)}, bf16[256,1024]{1,0:T(8,128)(2,1)}, bf16[256,128]{1,0:T(8,128)(2,1)}, f32[128,128]{1,0:T(8,128)}, s32[65]{0:T(128)S(1)}) custom-call(s32[16]{0:T(128)S(1)} %copy-done.10, s32[8,128]{1,0:T(8,128)} %bitcast.30, f32[8,128]{1,0:T(8,128)} %bitcast.31), custom_call_target="tpu_custom_call" | custom-call | tf_op jit(solution)/shard_map/route/pallas_call | solution.py:539
  89.7 2.6 %attn_own.1.own_ref = f32[128,2048]{1,0:T(8,128)S(1)} custom-call(bf16[512,512]{1,0:T(8,128)(2,1)S(1)} %get-tuple-element.39.q, bf16[1024,512]{1,0:T(8,128)(2,1)S(1)} %get-tuple-element.40.k, bf16[1024,512]{1,0:T(8,128)(2,1)S(1)} %get-tuple-element.41.v, bf16[1024,512]{1,0:T(8,128)(2,1)S(1)} %bitcast.18, bf16[1024,512]{1,0:T(8,128)(2,1)S(1)} %collective-permute-done.16.pb, ...), custom_call_target="tpu_custom_call" | custom-call | tf_op jit(solution)/shard_map/attn_own/pallas_call | solution.py:528
  92.3 3.6 %collective-permute-done.23.a1 = bf16[64,2048]{1,0:T(8,128)(2,1)S(1)} collective-permute-done((bf16[64,2048]{1,0:T(8,128)(2,1)S(1)}, bf16[64,2048]{1,0:T(8,128)(2,1)S(1)}, u32[]{:S(2)}, u32[]{:S(2)}) %collective-permute-start.23) | collective-permute-done | bytes 262176 | tf_op jit(solution)/shard_map/ppermute | solution.py:432
  96.0 1.8 dispatch.1
  97.8 61.5 %all_to_all.21.x_ref = bf16[64,16,2304]{2,1,0:T(8,128)(2,1)S(1)} all-to-all(bf16[64,16,2304]{2,1,0:T(8,128)(2,1)S(1)} %bitcast.19), channel_id=1, replica_groups=mesh['x'=4,'y'=4,'z'=4,'c'=2] {'x','y','z'}, dimensions={0} | all-to-all | bytes 9437184 | tf_op jit(solution)/shard_map/all_to_all | solution.py:556
  159.3 15.1 %ffn.1 = bf16[64,16,2304]{2,1,0:T(8,128)(2,1)S(1)} custom-call(s32[65]{0:T(128)S(1)} %get-tuple-element.33.order_ref, bf16[64,16,2304]{2,1,0:T(8,128)(2,1)S(1)} %all_to_all.21.x_ref, bf16[2048,512]{1,0:T(8,128)(2,1)S(1)} %bitcast.21, bf16[2048,512]{1,0:T(8,128)(2,1)S(1)} %bitcast.23, bf16[512,2048]{1,0:T(8,128)(2,1)S(1)} %bitcast.25, ...), custom_call_target="tpu_custom_call" | custom-call | tf_op jit(solution)/shard_map/ffn/pallas_call | solution.py:374
  174.5 63.4 %all_to_all.22 = bf16[64,16,2304]{2,1,0:T(8,128)(2,1)S(1)} all-to-all(bf16[64,16,2304]{2,1,0:T(8,128)(2,1)S(1)} %ffn.1), channel_id=1, replica_groups=mesh['x'=4,'y'=4,'z'=4,'c'=2] {'x','y','z'}, dimensions={0} | all-to-all | bytes 9437184 | tf_op jit(solution)/shard_map/all_to_all | solution.py:556
  237.9 2.4 combine.1
  (80 shorter events, 3.0 us)
Async XLA Ops:
  2.2 11.0 %collective-permute-start.2 = (bf16[64,2048]{1,0:T(8,128)(2,1)}, bf16[64,2048]{1,0:T(8,128)(2,1)S(1)}, u32[]{:S(2)}, u32[]{:S(2)}) collective-permute-start(bf16[64,2048]{1,0:T(8,128)(2,1)} %get-tuple-element.35), channel_id=1, source_target_pairs={{0,6},{2,0},{4,2},{6,4},{1,7},{3,1},{5,3},{7,5},{8,14},{10,8},{12,... | collective-permute-start | bytes 786440 | tf_op jit(solution)/shard_map/ppermute | solution.py:433
  6.2 10.6 %collective-permute-start = (bf16[64,2048]{1,0:T(8,128)(2,1)}, bf16[64,2048]{1,0:T(8,128)(2,1)S(1)}, u32[]{:S(2)}, u32[]{:S(2)}) collective-permute-start(bf16[64,2048]{1,0:T(8,128)(2,1)} %get-tuple-element.35), channel_id=1, source_target_pairs={{0,2},{2,4},{4,6},{6,0},{1,3},{3,5},{5,7},{7,1},{8,10},{10,12},{12... | collective-permute-start | bytes 786440 | tf_op jit(solution)/shard_map/ppermute | solution.py:432
  6.2 11.5 %collective-permute-start.3 = (bf16[64,2048]{1,0:T(8,128)(2,1)}, bf16[64,2048]{1,0:T(8,128)(2,1)S(1)}, u32[]{:S(2)}, u32[]{:S(2)}) collective-permute-start(bf16[64,2048]{1,0:T(8,128)(2,1)} %get-tuple-element.36), channel_id=1, source_target_pairs={{0,6},{2,0},{4,2},{6,4},{1,7},{3,1},{5,3},{7,5},{8,14},{10,8},{12,... | collective-permute-start | bytes 786440 | tf_op jit(solution)/shard_map/ppermute | solution.py:433
  9.4 11.6 %collective-permute-start.1 = (bf16[64,2048]{1,0:T(8,128)(2,1)}, bf16[64,2048]{1,0:T(8,128)(2,1)S(1)}, u32[]{:S(2)}, u32[]{:S(2)}) collective-permute-start(bf16[64,2048]{1,0:T(8,128)(2,1)} %get-tuple-element.36), channel_id=1, source_target_pairs={{0,2},{2,4},{4,6},{6,0},{1,3},{3,5},{5,7},{7,1},{8,10},{10,12},{12... | collective-permute-start | bytes 786440 | tf_op jit(solution)/shard_map/ppermute | solution.py:432
  13.2 7.8 %collective-permute-start.9 = (bf16[64,2048]{1,0:T(8,128)(2,1)S(1)}, bf16[64,2048]{1,0:T(8,128)(2,1)S(1)}, u32[]{:S(2)}, u32[]{:S(2)}) collective-permute-start(bf16[64,2048]{1,0:T(8,128)(2,1)S(1)} %collective-permute-done.2.refs_3_), channel_id=1, source_target_pairs={{0,1},{1,0},{2,3},{3,2},{4,5},{5,4},{6,7},{7,6},{8,9},{9,8},{10,11... | collective-permute-start | bytes 786440 | tf_op jit(solution)/shard_map/ppermute | solution.py:431
  16.8 4.7 %collective-permute-start.7 = (bf16[64,2048]{1,0:T(8,128)(2,1)S(1)}, bf16[64,2048]{1,0:T(8,128)(2,1)S(1)}, u32[]{:S(2)}, u32[]{:S(2)}) collective-permute-start(bf16[64,2048]{1,0:T(8,128)(2,1)S(1)} %collective-permute-done.refs_1_), channel_id=1, source_target_pairs={{0,1},{1,0},{2,3},{3,2},{4,5},{5,4},{6,7},{7,6},{8,9},{9,8},{10,11... | collective-permute-start | bytes 786440 | tf_op jit(solution)/shard_map/ppermute | solution.py:431
  16.8 10.0 %collective-permute-start.4 = (bf16[64,2048]{1,0:T(8,128)(2,1)S(1)}, bf16[64,2048]{1,0:T(8,128)(2,1)}, u32[]{:S(2)}, u32[]{:S(2)}) collective-permute-start(bf16[64,2048]{1,0:T(8,128)(2,1)S(1)} %collective-permute-done.refs_1_), channel_id=1, source_target_pairs={{0,2},{2,4},{4,6},{6,0},{1,3},{3,5},{5,7},{7,1},{8,10},{10,12},{12... | collective-permute-start | bytes 786440 | tf_op jit(solution)/shard_map/ppermute | solution.py:432
  17.7 25.0 %collective-permute-start.14 = (bf16[2048,256]{1,0:T(8,128)(2,1)}, bf16[2048,256]{1,0:T(8,128)(2,1)S(1)}, u32[]{:S(2)}, u32[]{:S(2)}) collective-permute-start(bf16[2048,256]{1,0:T(8,128)(2,1)} %refs_16_.1), channel_id=1, source_target_pairs={{0,1},{1,0},{2,3},{3,2},{4,5},{5,4},{6,7},{7,6},{8,9},{9,8},{10,11... | collective-permute-start | bytes 3145736 | tf_op jit(solution)/shard_map/ppermute | solution.py:431
  21.0 9.5 %collective-permute-start.6 = (bf16[128,2048]{1,0:T(8,128)(2,1)}, bf16[128,2048]{1,0:T(8,128)(2,1)S(1)}, u32[]{:S(2)}, u32[]{:S(2)}) collective-permute-start(bf16[128,2048]{1,0:T(8,128)(2,1)} %get-tuple-element.34.refs_0_), channel_id=1, source_target_pairs={{0,1},{1,0},{2,3},{3,2},{4,5},{5,4},{6,7},{7,6},{8,9},{9,8},{10,11... | collective-permute-start | bytes 1572872 | tf_op jit(solution)/shard_map/ppermute | solution.py:431
  21.0 5.8 %collective-permute-start.10 = (bf16[64,2048]{1,0:T(8,128)(2,1)S(1)}, bf16[64,2048]{1,0:T(8,128)(2,1)S(1)}, u32[]{:S(2)}, u32[]{:S(2)}) collective-permute-start(bf16[64,2048]{1,0:T(8,128)(2,1)S(1)} %collective-permute-done.3.refs_4_), channel_id=1, source_target_pairs={{0,1},{1,0},{2,3},{3,2},{4,5},{5,4},{6,7},{7,6},{8,9},{9,8},{10,11... | collective-permute-start | bytes 786440 | tf_op jit(solution)/shard_map/ppermute | solution.py:431
  21.5 8.4 %collective-permute-start.5 = (bf16[64,2048]{1,0:T(8,128)(2,1)S(1)}, bf16[64,2048]{1,0:T(8,128)(2,1)}, u32[]{:S(2)}, u32[]{:S(2)}) collective-permute-start(bf16[64,2048]{1,0:T(8,128)(2,1)S(1)} %collective-permute-done.3.refs_4_), channel_id=1, source_target_pairs={{0,6},{2,0},{4,2},{6,4},{1,7},{3,1},{5,3},{7,5},{8,14},{10,8},{12,... | collective-permute-start | bytes 786440 | tf_op jit(solution)/shard_map/ppermute | solution.py:433
  26.8 3.1 %collective-permute-start.8 = (bf16[64,2048]{1,0:T(8,128)(2,1)S(1)}, bf16[64,2048]{1,0:T(8,128)(2,1)S(1)}, u32[]{:S(2)}, u32[]{:S(2)}) collective-permute-start(bf16[64,2048]{1,0:T(8,128)(2,1)S(1)} %collective-permute-done.1.refs_2_), channel_id=1, source_target_pairs={{0,1},{1,0},{2,3},{3,2},{4,5},{5,4},{6,7},{7,6},{8,9},{9,8},{10,11... | collective-permute-start | bytes 786440 | tf_op jit(solution)/shard_map/ppermute | solution.py:431
  26.9 16.8 %collective-permute-start.13 = (bf16[2048,256]{1,0:T(8,128)(2,1)}, bf16[2048,256]{1,0:T(8,128)(2,1)}, u32[]{:S(2)}, u32[]{:S(2)}) collective-permute-start(bf16[2048,256]{1,0:T(8,128)(2,1)} %refs_14_.1), channel_id=1, source_target_pairs={{0,1},{1,0},{2,3},{3,2},{4,5},{5,4},{6,7},{7,6},{8,9},{9,8},{10,11... | collective-permute-start | bytes 3145736 | tf_op jit(solution)/shard_map/ppermute | solution.py:431
  29.9 27.1 %collective-permute-start.15 = (bf16[2048,256]{1,0:T(8,128)(2,1)}, bf16[2048,256]{1,0:T(8,128)(2,1)}, u32[]{:S(2)}, u32[]{:S(2)}) collective-permute-start(bf16[2048,256]{1,0:T(8,128)(2,1)} %refs_18_.1), channel_id=1, source_target_pairs={{0,1},{1,0},{2,3},{3,2},{4,5},{5,4},{6,7},{7,6},{8,9},{9,8},{10,11... | collective-permute-start | bytes 3145736 | tf_op jit(solution)/shard_map/ppermute | solution.py:431
  30.0 12.1 %collective-permute-start.11 = (bf16[64,2048]{1,0:T(8,128)(2,1)}, bf16[64,2048]{1,0:T(8,128)(2,1)}, u32[]{:S(2)}, u32[]{:S(2)}) collective-permute-start(bf16[64,2048]{1,0:T(8,128)(2,1)} %collective-permute-done.4.refs_5_), channel_id=1, source_target_pairs={{0,1},{1,0},{2,3},{3,2},{4,5},{5,4},{6,7},{7,6},{8,9},{9,8},{10,11... | collective-permute-start | bytes 786440 | tf_op jit(solution)/shard_map/ppermute | solution.py:431
  31.4 10.8 %collective-permute-start.12 = (bf16[64,2048]{1,0:T(8,128)(2,1)}, bf16[64,2048]{1,0:T(8,128)(2,1)}, u32[]{:S(2)}, u32[]{:S(2)}) collective-permute-start(bf16[64,2048]{1,0:T(8,128)(2,1)} %collective-permute-done.5.refs_6_), channel_id=1, source_target_pairs={{0,1},{1,0},{2,3},{3,2},{4,5},{5,4},{6,7},{7,6},{8,9},{9,8},{10,11... | collective-permute-start | bytes 786440 | tf_op jit(solution)/shard_map/ppermute | solution.py:431
  34.9 22.2 %all-to-all-start = ((bf16[16,64,512]{2,1,0:T(8,128)(2,1)}), bf16[16,64,512]{2,1,0:T(8,128)(2,1)S(1)}, u32[]{:S(2)}, u32[]{:S(2)}) async-start(bf16[16,64,512]{2,1,0:T(8,128)(2,1)} %bitcast.28), calls=%async_computation | async-start | bytes 2097152 | tf_op jit(solution)/shard_map/all_to_all | solution.py:464
  42.1 39.6 %collective-permute-start.18 = (bf16[2048,512]{1,0:T(8,128)(2,1)}, bf16[2048,512]{1,0:T(8,128)(2,1)}, u32[]{:S(2)}, u32[]{:S(2)}) collective-permute-start(bf16[2048,512]{1,0:T(8,128)(2,1)} %bitcast.20), channel_id=1, source_target_pairs={{0,1},{1,0},{2,3},{3,2},{4,5},{5,4},{6,7},{7,6},{8,9},{9,8},{10,11... | collective-permute-start | bytes 6291464 | tf_op jit(solution)/shard_map/ppermute | solution.py:431
  42.2 39.8 %collective-permute-start.19 = (bf16[2048,512]{1,0:T(8,128)(2,1)}, bf16[2048,512]{1,0:T(8,128)(2,1)}, u32[]{:S(2)}, u32[]{:S(2)}) collective-permute-start(bf16[2048,512]{1,0:T(8,128)(2,1)} %bitcast.22), channel_id=1, source_target_pairs={{0,1},{1,0},{2,3},{3,2},{4,5},{5,4},{6,7},{7,6},{8,9},{9,8},{10,11... | collective-permute-start | bytes 6291464 | tf_op jit(solution)/shard_map/ppermute | solution.py:431
  42.7 49.6 %collective-permute-start.20 = (bf16[512,2048]{1,0:T(8,128)(2,1)}, bf16[512,2048]{1,0:T(8,128)(2,1)}, u32[]{:S(2)}, u32[]{:S(2)}) collective-permute-start(bf16[512,2048]{1,0:T(8,128)(2,1)} %bitcast.24), channel_id=1, source_target_pairs={{0,1},{1,0},{2,3},{3,2},{4,5},{5,4},{6,7},{7,6},{8,9},{9,8},{10,11... | collective-permute-start | bytes 6291464 | tf_op jit(solution)/shard_map/ppermute | solution.py:431
  43.7 23.4 %collective-permute-start.17 = (bf16[256,2048]{1,0:T(8,128)(2,1)S(1)}, bf16[256,2048]{1,0:T(8,128)(2,1)S(1)}, u32[]{:S(2)}, u32[]{:S(2)}) collective-permute-start(bf16[256,2048]{1,0:T(8,128)(2,1)S(1)} %copy-done), channel_id=1, source_target_pairs={{0,1},{1,0},{2,3},{3,2},{4,5},{5,4},{6,7},{7,6},{8,9},{9,8},{10,11... | collective-permute-start | bytes 3145736 | tf_op jit(solution)/shard_map/ppermute | solution.py:431
  57.1 10.0 %collective-permute-start.16 = (bf16[1024,512]{1,0:T(8,128)(2,1)S(1)}, bf16[1024,512]{1,0:T(8,128)(2,1)S(1)}, u32[]{:S(2)}, u32[]{:S(2)}) collective-permute-start(bf16[1024,512]{1,0:T(8,128)(2,1)S(1)} %bitcast.15), channel_id=1, source_target_pairs={{0,1},{1,0},{2,3},{3,2},{4,5},{5,4},{6,7},{7,6},{8,9},{9,8},{10,11... | collective-permute-start | bytes 3145736 | tf_op jit(solution)/shard_map/ppermute | solution.py:431
  69.7 8.8 %collective-permute-start.21 = (bf16[64,2048]{1,0:T(8,128)(2,1)S(1)}, bf16[64,2048]{1,0:T(8,128)(2,1)S(1)}, u32[]{:S(2)}, u32[]{:S(2)}) collective-permute-start(bf16[64,2048]{1,0:T(8,128)(2,1)S(1)} %get-tuple-element.45), channel_id=1, source_target_pairs={{0,6},{2,0},{4,2},{6,4},{1,7},{3,1},{5,3},{7,5},{8,14},{10,8},{12,... | collective-permute-start | bytes 786440 | tf_op jit(solution)/shard_map/ppermute | solution.py:433
  71.7 9.9 %collective-permute-start.22 = (bf16[64,2048]{1,0:T(8,128)(2,1)S(1)}, bf16[64,2048]{1,0:T(8,128)(2,1)S(1)}, u32[]{:S(2)}, u32[]{:S(2)}) collective-permute-start(bf16[64,2048]{1,0:T(8,128)(2,1)S(1)} %get-tuple-element.47), channel_id=1, source_target_pairs={{0,2},{2,4},{4,6},{6,0},{1,3},{3,5},{5,7},{7,1},{8,10},{10,12},{12... | collective-permute-start | bytes 786440 | tf_op jit(solution)/shard_map/ppermute | solution.py:432
  78.4 13.9 %collective-permute-start.24 = (bf16[64,2048]{1,0:T(8,128)(2,1)S(1)}, bf16[64,2048]{1,0:T(8,128)(2,1)S(1)}, u32[]{:S(2)}, u32[]{:S(2)}) collective-permute-start(bf16[64,2048]{1,0:T(8,128)(2,1)S(1)} %get-tuple-element.49), channel_id=1, source_target_pairs={{0,6},{2,0},{4,2},{6,4},{1,7},{3,1},{5,3},{7,5},{8,14},{10,8},{12,... | collective-permute-start | bytes 786440 | tf_op jit(solution)/shard_map/ppermute | solution.py:433
  81.6 10.8 %collective-permute-start.25 = (bf16[64,2048]{1,0:T(8,128)(2,1)S(1)}, bf16[64,2048]{1,0:T(8,128)(2,1)S(1)}, u32[]{:S(2)}, u32[]{:S(2)}) collective-permute-start(bf16[64,2048]{1,0:T(8,128)(2,1)S(1)} %get-tuple-element.50), channel_id=1, source_target_pairs={{0,2},{2,4},{4,6},{6,0},{1,3},{3,5},{5,7},{7,1},{8,10},{10,12},{12... | collective-permute-start | bytes 786440 | tf_op jit(solution)/shard_map/ppermute | solution.py:432
  81.7 14.3 %collective-permute-start.23 = (bf16[64,2048]{1,0:T(8,128)(2,1)S(1)}, bf16[64,2048]{1,0:T(8,128)(2,1)S(1)}, u32[]{:S(2)}, u32[]{:S(2)}) collective-permute-start(bf16[64,2048]{1,0:T(8,128)(2,1)S(1)} %get-tuple-element.48), channel_id=1, source_target_pairs={{0,2},{2,4},{4,6},{6,0},{1,3},{3,5},{5,7},{7,1},{8,10},{10,12},{12... | collective-permute-start | bytes 786440 | tf_op jit(solution)/shard_map/ppermute | solution.py:432
  82.0 14.0 %collective-permute-start.26 = (bf16[64,2048]{1,0:T(8,128)(2,1)S(1)}, bf16[64,2048]{1,0:T(8,128)(2,1)S(1)}, u32[]{:S(2)}, u32[]{:S(2)}) collective-permute-start(bf16[64,2048]{1,0:T(8,128)(2,1)S(1)} %get-tuple-element.51), channel_id=1, source_target_pairs={{0,6},{2,0},{4,2},{6,4},{1,7},{3,1},{5,3},{7,5},{8,14},{10,8},{12,... | collective-permute-start | bytes 786440 | tf_op jit(solution)/shard_map/ppermute | solution.py:433
  174.4 63.4 %copy-start.5 = (bf16[256,1024]{1,0:T(8,128)(2,1)S(1)}, bf16[256,1024]{1,0:T(8,128)(2,1)}, u32[]{:S(2)}) copy-start(bf16[256,1024]{1,0:T(8,128)(2,1)} %get-tuple-element.57.wm_ref) | copy-start | bytes 1572868
  174.5 63.4 %copy-start.6 = (bf16[128,2048]{1,0:T(8,128)(2,1)S(1)}, bf16[128,2048]{1,0:T(8,128)(2,1)}, u32[]{:S(2)}) copy-start(bf16[128,2048]{1,0:T(8,128)(2,1)} %get-tuple-element.59.h_ref) | copy-start | bytes 1572868
  174.5 63.4 %copy-start.7 = (bf16[256,128]{1,0:T(8,128)(2,1)S(1)}, bf16[256,128]{1,0:T(8,128)(2,1)}, u32[]{:S(2)}) copy-start(bf16[256,128]{1,0:T(8,128)(2,1)} %get-tuple-element.58.wx_ref) | copy-start | bytes 196612
  174.5 63.4 %copy-start.8 = (f32[128,128]{1,0:T(8,128)S(1)}, f32[128,128]{1,0:T(8,128)}, u32[]{:S(2)}) copy-start(f32[128,128]{1,0:T(8,128)} %get-tuple-element.60.live_ref) | copy-start | bytes 196612
  (17 other events, 325.7 us)
